TPU v7x, 256 devices: a whole 4x4x8 slice. The times are simulated.
256 devices in a mesh: dp: 64 (over x_lo, y, z), ep: 4 (over x_hi, core).
Axes of the slice: x: 4 (x_hi: 2, x_lo: 2; x = x_hi * 2 + x_lo), y: 4, z: 8, core: 2. Of those that a mesh axis runs over, the one named last changes fastest.
Arguments:
- tokens: bfloat16 [1024, 4096], P(('dp', 'ep')), may hold values from -6 to 6
- router: float32 [4096, 8], replicated, may hold values from -0.1875 to 0.1875
- expert_ids: int32 [1024, 2], P(('dp', 'ep')), may hold values from 0 to 7, all different within a row; in each aligned block of 4 rows (0 to 3, 4 to 7, ...) at most 2 rows name the same one
- w_gate: bfloat16 [64, 4096, 1536], P('dp', None, 'ep'), may hold values from -0.09375 to 0.09375
- w_up: bfloat16 [64, 4096, 1536], P('dp', None, 'ep'), may hold values from -0.09375 to 0.09375
- w_down: bfloat16 [64, 1536, 4096], P('dp', 'ep'), may hold values from -0.0546875 to 0.0546875
- states: bfloat16 [1024, 16, 8192], P('dp', None, 'ep'), may hold values from -6 to 6
- kv_blocks: bfloat16 [2048, 2, 16, 1024], P('dp', None, None, 'ep'), may hold values from -6 to 6
- plan_slots: int32 [64, 2, 3], replicated, may hold values from -1 to 63, as said below
- plan_len: int32 [64, 2], replicated, may hold values from 0 to 32, as said below
- plan_blocks: int32 [64, 2, 2, 2], replicated, may hold values from -1 to 31, as said below
Outputs:
- mixed: bfloat16 [1024, 4096], P(('dp', 'ep'))
- new_states: bfloat16 [1024, 16, 8192], P('dp', None, 'ep')
- new_cache: bfloat16 [2048, 2, 16, 1024], P('dp', None, None, 'ep')
Inputs may be any that keep to these rules, and one draw needn't show every extreme that they name: `expert_ids`: in the rows of one device no expert is named more than 2 times. `plan_slots`: A move is live exactly where its first entry is not -1, and then all three entries are set; otherwise all are -1. For each m there is one distance d_m from 1 to 63, distinct for distinct m, such that every live move (r, m) goes to rank (r + d_m) mod 64. The leaving slots of a rank are distinct, the slots taken at a rank are distinct and differ from its leaving slots. Some rank has all 2 moves live. `plan_len`: zero exactly where the move is not live; some move holds 32 tokens. `plan_blocks`: entry j of both tables is -1 exactly where j * 16 >= plan_len. The blocks leaving a rank are distinct, the blocks taken at a rank are distinct and differ from the ones leaving it.
All inputs are finite; a program needn't handle non-finite values.
Results may differ from a plain program's by a relative error of at most 0.005.
Values may be sent and summed in bfloat16 or wider, within the bound.
No kernel may reach another device: no remote copies, remote signals or barrier semaphores. Data moves between devices by JAX's collectives and lax.ppermute only.
A program may use at most 128 MiB of HBM per device.

v0:
```python
import jax
import jax.numpy as jnp
from jax import lax
from jax.sharding import PartitionSpec as P

CAP = 2


def passed_along(value, axis, steps):
    count = lax.axis_size(axis)
    pairs = [(source, (source + steps) % count) for source in range(count)]
    return lax.ppermute(value, axis, pairs)


def hop_along(item_pair, distance, ranks):
    steps_needed = (ranks - 1).bit_length()
    for level in range(steps_needed):
        moved = passed_along((item_pair[0], item_pair[1]), "dp", 1 << level)
        taken = distance >> level & 1 == 1
        item_pair = (
            jnp.where(taken, moved[0], item_pair[0]),
            jnp.where(taken, moved[1], item_pair[1]),
        )
    return item_pair


def local(
    tokens,
    router,
    expert_ids,
    w_gate,
    w_up,
    w_down,
    states,
    kv_blocks,
    plan_slots,
    plan_len,
    plan_blocks,
):
    ranks = lax.axis_size("dp")
    here = lax.axis_index("dp")
    moves = plan_slots.shape[1]
    slot_count = states.shape[0]
    block_count = kv_blocks.shape[0]
    per_request = plan_blocks.shape[3]
    block_len = kv_blocks.shape[2]
    mine = lax.dynamic_index_in_dim(plan_slots, here, 0, keepdims=False)
    my_blocks = lax.dynamic_index_in_dim(plan_blocks, here, 0, keepdims=False)
    my_length = lax.dynamic_index_in_dim(plan_len, here, 0, keepdims=False)
    leaving_slot = mine[:, 0]
    leaving_block = my_blocks[:, 0, :]
    state_out = states[jnp.maximum(leaving_slot, 0)]
    state_out = jnp.where((leaving_slot >= 0)[:, None, None], state_out, jnp.zeros_like(state_out))
    cache_out = kv_blocks[jnp.maximum(leaving_block, 0)]
    position = jnp.arange(per_request)[:, None] * block_len + jnp.arange(block_len)[None, :]
    written = (leaving_block >= 0)[:, :, None] & (position[None] < my_length[:, None, None])
    cache_out = jnp.where(written[:, :, None, :, None], cache_out, jnp.zeros_like(cache_out))
    arrivals = plan_slots[:, :, 1] == here
    sender = jnp.sum(jnp.where(arrivals, jnp.arange(ranks)[:, None], 0), axis=0)
    arriving = jnp.any(arrivals, axis=0)
    rank_line = jnp.arange(ranks, dtype=jnp.int32)
    live_all = plan_slots[:, :, 0] >= 0
    span = jnp.where(live_all, (plan_slots[:, :, 1] - rank_line[:, None]) % ranks, 0)
    distance_of = jnp.max(span, axis=0)
    state_list = []
    cache_list = []
    for move_index in range(moves):
        got = hop_along(
            (state_out[move_index], cache_out[move_index]), distance_of[move_index], ranks
        )
        state_list.append(got[0])
        cache_list.append(got[1])
    state_in = jnp.stack(state_list, axis=0)
    cache_in = jnp.stack(cache_list, axis=0)
    slot_line = jnp.arange(slot_count)
    gone = jnp.any(slot_line[:, None] == leaving_slot[None, :], axis=1)
    new_states = jnp.where(gone[:, None, None], jnp.zeros_like(states), states)
    block_line = jnp.arange(block_count)
    gone_blocks = jnp.any(block_line[:, None, None] == leaving_block[None], axis=(1, 2))
    new_cache = jnp.where(gone_blocks[:, None, None, None], jnp.zeros_like(kv_blocks), kv_blocks)
    for move_index in range(moves):
        anchor = sender[move_index]
        place = plan_slots[anchor, move_index, 2]
        landing = (slot_line == place) & arriving[move_index]
        new_states = jnp.where(landing[:, None, None], state_in[move_index][None], new_states)
        for block_index in range(per_request):
            spot = plan_blocks[anchor, move_index, 1, block_index]
            block_hit = (block_line == spot) & arriving[move_index]
            new_cache = jnp.where(
                block_hit[:, None, None, None], cache_in[move_index, block_index][None], new_cache
            )
    experts = router.shape[1]
    tok_count = tokens.shape[0]
    width = tokens.shape[1]
    group = ranks // experts
    flat_ids = expert_ids.reshape(-1)
    onehot = (flat_ids[:, None] == jnp.arange(experts)[None, :]).astype(jnp.int32)
    earlier = jnp.cumsum(onehot, axis=0) - onehot
    slot_of = jnp.sum(earlier * onehot, axis=1)
    target_row = flat_ids * CAP + slot_of
    placer = (jnp.arange(experts * CAP)[:, None] == target_row[None, :]).astype(jnp.bfloat16)
    doubled = jnp.repeat(tokens, 2, axis=0)
    packed = jnp.dot(placer, doubled, preferred_element_type=jnp.float32).astype(jnp.bfloat16)
    outgoing = jnp.repeat(packed.reshape(experts, CAP, width), group, axis=0)
    incoming = lax.all_to_all(outgoing, "dp", split_axis=0, concat_axis=0, tiled=True)
    rows_in = incoming.reshape(ranks * CAP, width)
    piece = lax.all_gather(rows_in, "ep", axis=0, tiled=True)
    gate = jnp.dot(piece, w_gate[0], preferred_element_type=jnp.float32)
    upper = jnp.dot(piece, w_up[0], preferred_element_type=jnp.float32)
    hidden = (jax.nn.silu(gate) * upper).astype(jnp.bfloat16)
    summed = lax.psum_scatter(
        jnp.dot(hidden, w_down[0], preferred_element_type=jnp.float32),
        "ep",
        scatter_dimension=0,
        tiled=True,
    )
    returned = lax.all_to_all(
        summed.reshape(ranks, CAP, width), "dp", split_axis=0, concat_axis=0, tiled=True
    )
    expert_out = jnp.sum(returned.reshape(experts, group, CAP, width), axis=1).reshape(
        experts * CAP, width
    )
    chosen = expert_out[target_row].reshape(tok_count, 2, width)
    logits = jnp.dot(tokens.astype(jnp.float32), router, precision=lax.Precision.HIGHEST)
    scores = jax.nn.sigmoid(jnp.take_along_axis(logits, expert_ids, axis=1))
    weights = scores / jnp.sum(scores, axis=1, keepdims=True)
    mixed = jnp.sum(weights[:, :, None] * chosen, axis=1).astype(jnp.bfloat16)
    return (mixed, new_states, new_cache)


def solution(mesh):
    placed = (
        P(("dp", "ep"), None),
        P(),
        P(("dp", "ep"), None),
        P("dp", None, "ep"),
        P("dp", None, "ep"),
        P("dp", "ep", None),
        P("dp", None, "ep"),
        P("dp", None, None, "ep"),
        P(),
        P(),
        P(),
    )
    return jax.shard_map(
        local,
        mesh=mesh,
        in_specs=placed,
        out_specs=(P(("dp", "ep"), None), P("dp", None, "ep"), P("dp", None, None, "ep")),
        check_vma=False,
    )
```

profile of v0, /device:TPU:34, one launch (start us, length us, event | category | flops | bytes accessed | tf_op | source)
XLA Modules:
  0.0 283.0 jit_solution(17758954699944343621)
XLA Ops:
  7.2 0.9 broadcast_in_dim.175
  8.2 0.8 copy.30
  9.4 0.5 copy-done.6
  10.1 1.0 broadcast_in_dim.176
  11.1 42.1 %all_to_all.10 = bf16[64,2,4096]{2,1,0:T(2,128)(2,1)} all-to-all(bf16[64,2,4096]{2,1,0:T(2,128)(2,1)S(1)} %bitcast.101), channel_id=1, replica_groups=mesh['dp'=64,'ep'=4] {'dp'}, dimensions={0} | all-to-all | bytes 2097152 | tf_op jit(solution)/shard_map/all_to_all | solution.py:105
  53.2 2.2 reshape.263
  55.6 36.1 %all-gather.2.cloned.1.call-done = bf16[512,4096]{1,0:T(8,128)(2,1)} async-done(((bf16[128,4096]{1,0:T(8,128)(2,1)}), bf16[512,4096]{1,0:T(8,128)(2,1)}) %all-gather.2.cloned.1.call-update) | async-done | bytes 4194320 | tf_op jit(solution)/shard_map/all_gather | solution.py:107
  91.7 6.4 %fusion.4 = f32[512,384]{1,0:T(8,128)} fusion(bf16[512,4096]{1,0:T(8,128)(2,1)} %all-gather.2.cloned.1.call-done, bf16[1,4096,384]{2,1,0:T(8,128)(2,1)} %param.14), kind=kOutput, calls=%fused_computation.9 | convolution fusion | flops 1610612736 | bytes 8126464 | tf_op jit(solution)/shard_map/dot_general | solution.py:108
  98.1 11.0 %fusion = f32[512,4096]{1,0:T(8,128)} fusion(bf16[1,384,4096]{2,1,0:T(8,128)(2,1)S(1)} %copy-done, bf16[512,4096]{1,0:T(8,128)(2,1)} %all-gather.2.cloned.1.call-done, bf16[1,4096,384]{2,1,0:T(8,128)(2,1)} %param.15, f32[512,384]{1,0:T(8,128)} %fusion.4), kind=kOutput, calls=%fused_computation.5 | convolution fusion | flops 3222405120 | bytes 19660800 | tf_op jit(solution)/shard_map/dot_general | solution.py:112
  109.1 0.6 copy-done.3
  110.1 1.8 gather_fusion.1
  112.0 0.7 slice_bitcast_fusion.1
  112.7 1.6 collective-permute-start
  114.2 1.6 collective-permute-start.6
  116.1 0.9 fusion.22
  117.0 1.6 gather_fusion.2
  118.8 0.6 slice_bitcast_fusion.3
  119.5 2.8 collective-permute-start.12
  122.2 0.7 collective-permute-start.18
  123.0 0.6 fusion.29
  126.7 1.0 fusion.31
  127.7 0.7 gather_fusion.3
  129.8 0.6 constant_dynamic-slice_fusion.7
  130.4 0.7 constant_dynamic-slice_fusion.6
  131.2 0.7 fusion.30
  131.8 1.7 compare_and_fusion.1
  133.6 2.5 compare_and_fusion.5
  136.1 0.6 fusion.25
  136.7 0.6 fusion.28
  137.4 0.7 compare_reduce_fusion.1
  138.1 0.8 compare_reduce_fusion
  138.9 2.0 compare_and_fusion.3
  147.9 0.8 collective-permute-start.19
  148.8 1.8 collective-permute-start.13
  150.6 0.9 broadcast_select_fusion.8
  151.5 2.6 collective-permute-start.7
  154.1 2.8 %collective-permute-start.1 = (bf16[16,2048]{1,0:T(8,128)(2,1)S(1)}, bf16[16,2048]{1,0:T(8,128)(2,1)S(1)}, u32[]{:S(2)}, u32[]{:S(2)}) collective-permute-start(bf16[16,2048]{1,0:T(8,128)(2,1)S(1)} %get-tuple-element.7), channel_id=1, source_target_pairs={{0,8},{4,12},{8,16},{12,20},{16,24},{20,28},{24,32},{28,36},{32,40... | collective-permute-start | bytes 196616 | tf_op jit(solution)/shard_map/ppermute | solution.py:12
  157.2 1.9 collective-permute-start.20
  159.1 4.9 %collective-permute-start.14 = (bf16[2,2,16,256]{3,2,1,0:T(8,128)(2,1)S(1)}, bf16[2,2,16,256]{3,2,1,0:T(8,128)(2,1)S(1)}, u32[]{:S(2)}, u32[]{:S(2)}) collective-permute-start(bf16[2,2,16,256]{3,2,1,0:T(8,128)(2,1)S(1)} %broadcast_select_fusion.20), channel_id=1, source_target_pairs={{0,16},{4,20},{8,24},{12,28},{16,32},{20,36},{24,40},{28,44},{32,4... | collective-permute-start | bytes 98312 | tf_op jit(solution)/shard_map/ppermute | solution.py:12
  164.0 4.5 %collective-permute-done.20 = bf16[2,2,16,256]{3,2,1,0:T(8,128)(2,1)S(1)} collective-permute-done((bf16[2,2,16,256]{3,2,1,0:T(8,128)(2,1)S(1)}, bf16[2,2,16,256]{3,2,1,0:T(8,128)(2,1)S(1)}, u32[]{:S(2)}, u32[]{:S(2)}) %collective-permute-start.20) | collective-permute-done | bytes 32800 | tf_op jit(solution)/shard_map/ppermute | solution.py:12
  168.6 1.5 collective-permute-done.14
  170.2 3.3 %collective-permute-start.8 = (bf16[16,2048]{1,0:T(8,128)(2,1)S(1)}, bf16[16,2048]{1,0:T(8,128)(2,1)S(1)}, u32[]{:S(2)}, u32[]{:S(2)}) collective-permute-start(bf16[16,2048]{1,0:T(8,128)(2,1)S(1)} %broadcast_select_fusion.3), channel_id=1, source_target_pairs={{0,16},{4,20},{8,24},{12,28},{16,32},{20,36},{24,40},{28,44},{32,4... | collective-permute-start | bytes 196616 | tf_op jit(solution)/shard_map/ppermute | solution.py:12
  173.6 2.6 collective-permute-start.2
  176.1 5.7 %collective-permute-start.22 = (bf16[2,2,16,256]{3,2,1,0:T(8,128)(2,1)S(1)}, bf16[2,2,16,256]{3,2,1,0:T(8,128)(2,1)S(1)}, u32[]{:S(2)}, u32[]{:S(2)}) collective-permute-start(bf16[2,2,16,256]{3,2,1,0:T(8,128)(2,1)S(1)} %broadcast_select_fusion.17), channel_id=1, source_target_pairs={{0,64},{4,68},{8,72},{12,76},{16,80},{20,84},{24,88},{28,92},{32,9... | collective-permute-start | bytes 98312 | tf_op jit(solution)/shard_map/ppermute | solution.py:12
  182.0 2.0 collective-permute-done.22
  184.0 2.3 collective-permute-start.23
  186.3 2.6 collective-permute-done.16
  189.2 0.5 collective-permute-start.9
  189.8 3.7 %reduce-scatter.2.cloned.1.call-done = f32[128,4096]{1,0:T(8,128)} async-done(((f32[512,4096]{1,0:T(8,128)}), f32[128,4096]{1,0:T(8,128)}) %reduce-scatter.2.cloned.1.call-update) | async-done | bytes 2097168 | tf_op jit(solution)/shard_map/reduce_scatter | solution.py:111
  193.5 3.5 %reshape.264 = f32[64,2,4096]{2,1,0:T(2,128)} reshape(f32[128,4096]{1,0:T(8,128)} %reduce-scatter.2.cloned.1.call-done) | data formatting | bytes 4194304 | tf_op jit(solution)/shard_map/reshape | solution.py:118
  197.0 21.6 %all-to-all-start.1 = ((f32[64,2,4096]{2,1,0:T(2,128)}), f32[64,2,4096]{2,1,0:T(2,128)}, u32[]{:S(2)}, u32[]{:S(2)}) async-start(f32[64,2,4096]{2,1,0:T(2,128)} %reshape.264), calls=%async_computation.2 | async-start | bytes 4194304 | tf_op jit(solution)/shard_map/all_to_all | solution.py:117
  218.7 2.2 select_select_fusion.1
  220.9 3.2 %collective-permute-start.10 = (bf16[16,2048]{1,0:T(8,128)(2,1)S(1)}, bf16[16,2048]{1,0:T(8,128)(2,1)S(1)}, u32[]{:S(2)}, u32[]{:S(2)}) collective-permute-start(bf16[16,2048]{1,0:T(8,128)(2,1)S(1)} %broadcast_select_fusion.5), channel_id=1, source_target_pairs={{0,64},{4,68},{8,72},{12,76},{16,80},{20,84},{24,88},{28,92},{32,9... | collective-permute-start | bytes 196616 | tf_op jit(solution)/shard_map/ppermute | solution.py:12
  224.0 0.4 collective-permute-start.4
  224.5 3.5 %collective-permute-done.10 = bf16[16,2048]{1,0:T(8,128)(2,1)S(1)} collective-permute-done((bf16[16,2048]{1,0:T(8,128)(2,1)S(1)}, bf16[16,2048]{1,0:T(8,128)(2,1)S(1)}, u32[]{:S(2)}, u32[]{:S(2)}) %collective-permute-start.10) | collective-permute-done | bytes 65568 | tf_op jit(solution)/shard_map/ppermute | solution.py:12
  228.0 2.0 collective-permute-start.11
  230.0 3.7 %collective-permute-done.4 = bf16[16,2048]{1,0:T(8,128)(2,1)S(1)} collective-permute-done((bf16[16,2048]{1,0:T(8,128)(2,1)S(1)}, bf16[16,2048]{1,0:T(8,128)(2,1)S(1)}, u32[]{:S(2)}, u32[]{:S(2)}) %collective-permute-start.4) | collective-permute-done | bytes 65568 | tf_op jit(solution)/shard_map/ppermute | solution.py:12
  233.8 4.5 %collective-permute-done.5 = bf16[16,2048]{1,0:T(8,128)(2,1)S(1)} collective-permute-done((bf16[16,2048]{1,0:T(8,128)(2,1)S(1)}, bf16[16,2048]{1,0:T(8,128)(2,1)S(1)}, u32[]{:S(2)}, u32[]{:S(2)}) %collective-permute-start.5) | collective-permute-done | bytes 65568 | tf_op jit(solution)/shard_map/ppermute | solution.py:12
  238.3 1.3 select_select_fusion
  239.6 30.9 %all-to-all-done.1 = f32[64,2,4096]{2,1,0:T(2,128)} async-done(((f32[64,2,4096]{2,1,0:T(2,128)}), f32[64,2,4096]{2,1,0:T(2,128)}, u32[]{:S(2)}, u32[]{:S(2)}) %all-to-all-start.1) | async-done | bytes 2097184 | tf_op jit(solution)/shard_map/all_to_all | solution.py:117
  270.5 3.0 %bitcast_reduce_fusion = f32[8,2,4096]{2,1,0:T(2,128)} fusion(f32[64,2,4096]{2,1,0:T(2,128)} %all-to-all-done.1), kind=kLoop, calls=%fused_computation.11 | loop fusion | flops 458752 | bytes 2359296 | tf_op jit(solution)/shard_map/reduce_sum | solution.py:120
  273.5 1.1 reshape.266
  274.6 0.6 gather_fusion
  275.3 0.9 multiply_reduce_fusion
  (100 shorter events, 3.9 us)
Async XLA Ops:
  7.2 90.9 %copy-start = (bf16[1,384,4096]{2,1,0:T(8,128)(2,1)S(1)}, bf16[1,384,4096]{2,1,0:T(8,128)(2,1)}, u32[]{:S(2)}) copy-start(bf16[1,384,4096]{2,1,0:T(8,128)(2,1)} %param.16) | copy-start | bytes 9437188
  7.2 84.5 %all-gather.2.cloned.1.call-start = ((), (), s32[]{:S(2)}) async-start(), calls=%async_computation.3 | async-start | bytes 5242880 | tf_op jit(solution)/shard_map/all_gather | solution.py:107
  9.4 0.5 copy-start.6
  55.5 138.0 %reduce-scatter.2.cloned.1.call-start = ((), (), s32[]{:S(2)}) async-start(), calls=%async_computation.4 | async-start | bytes 10485760 | tf_op jit(solution)/shard_map/reduce_scatter | solution.py:111
  109.1 0.7 copy-start.3
  109.1 6.7 %copy-start.4 = (s32[64,2,2,2]{0,3,2,1:T(2,128)S(1)}, s32[64,2,2,2]{0,3,2,1:T(2,128)}, u32[]{:S(2)}) copy-start(s32[64,2,2,2]{0,3,2,1:T(2,128)} %param.21) | copy-start | bytes 6148
  109.1 17.6 %copy-start.2 = (f32[4096,8]{0,1:T(8,128)S(1)}, f32[4096,8]{0,1:T(8,128)}, u32[]{:S(2)}) copy-start(f32[4096,8]{0,1:T(8,128)} %param.12) | copy-start | bytes 393220
  110.1 1.8 copy-start.7
  112.7 37.9 %collective-permute-start = (bf16[16,2048]{1,0:T(8,128)(2,1)}, bf16[16,2048]{1,0:T(8,128)(2,1)}, u32[]{:S(2)}, u32[]{:S(2)}) collective-permute-start(bf16[16,2048]{1,0:T(8,128)(2,1)} %get-tuple-element.9), channel_id=1, source_target_pairs={{0,4},{4,8},{8,12},{12,16},{16,20},{20,24},{24,28},{28,32},{32,36}... | collective-permute-start | bytes 196616 | tf_op jit(solution)/shard_map/ppermute | solution.py:12
  114.2 36.4 %collective-permute-start.6 = (bf16[16,2048]{1,0:T(8,128)(2,1)}, bf16[16,2048]{1,0:T(8,128)(2,1)}, u32[]{:S(2)}, u32[]{:S(2)}) collective-permute-start(bf16[16,2048]{1,0:T(8,128)(2,1)} %get-tuple-element.10), channel_id=1, source_target_pairs={{0,4},{4,8},{8,12},{12,16},{16,20},{20,24},{24,28},{28,32},{32,36}... | collective-permute-start | bytes 196616 | tf_op jit(solution)/shard_map/ppermute | solution.py:12
  116.0 2.7 copy-start.5
  119.5 28.4 %collective-permute-start.12 = (bf16[2,2,16,256]{3,2,1,0:T(8,128)(2,1)}, bf16[2,2,16,256]{3,2,1,0:T(8,128)(2,1)S(1)}, u32[]{:S(2)}, u32[]{:S(2)}) collective-permute-start(bf16[2,2,16,256]{3,2,1,0:T(8,128)(2,1)} %get-tuple-element.13), channel_id=1, source_target_pairs={{0,4},{4,8},{8,12},{12,16},{16,20},{20,24},{24,28},{28,32},{32,36}... | collective-permute-start | bytes 98312 | tf_op jit(solution)/shard_map/ppermute | solution.py:12
  122.2 25.7 %collective-permute-start.18 = (bf16[2,2,16,256]{3,2,1,0:T(8,128)(2,1)}, bf16[2,2,16,256]{3,2,1,0:T(8,128)(2,1)}, u32[]{:S(2)}, u32[]{:S(2)}) collective-permute-start(bf16[2,2,16,256]{3,2,1,0:T(8,128)(2,1)} %get-tuple-element.14), channel_id=1, source_target_pairs={{0,4},{4,8},{8,12},{12,16},{16,20},{20,24},{24,28},{28,32},{32,36}... | collective-permute-start | bytes 98312 | tf_op jit(solution)/shard_map/ppermute | solution.py:12
  147.9 9.2 %collective-permute-start.19 = (bf16[2,2,16,256]{3,2,1,0:T(8,128)(2,1)S(1)}, bf16[2,2,16,256]{3,2,1,0:T(8,128)(2,1)S(1)}, u32[]{:S(2)}, u32[]{:S(2)}) collective-permute-start(bf16[2,2,16,256]{3,2,1,0:T(8,128)(2,1)S(1)} %get-tuple-element.12), channel_id=1, source_target_pairs={{0,8},{4,12},{8,16},{12,20},{16,24},{20,28},{24,32},{28,36},{32,40... | collective-permute-start | bytes 98312 | tf_op jit(solution)/shard_map/ppermute | solution.py:12
  148.8 10.3 %collective-permute-start.13 = (bf16[2,2,16,256]{3,2,1,0:T(8,128)(2,1)S(1)}, bf16[2,2,16,256]{3,2,1,0:T(8,128)(2,1)S(1)}, u32[]{:S(2)}, u32[]{:S(2)}) collective-permute-start(bf16[2,2,16,256]{3,2,1,0:T(8,128)(2,1)S(1)} %get-tuple-element.11), channel_id=1, source_target_pairs={{0,8},{4,12},{8,16},{12,20},{16,24},{20,28},{24,32},{28,36},{32,40... | collective-permute-start | bytes 98312 | tf_op jit(solution)/shard_map/ppermute | solution.py:12
  151.5 18.7 %collective-permute-start.7 = (bf16[16,2048]{1,0:T(8,128)(2,1)S(1)}, bf16[16,2048]{1,0:T(8,128)(2,1)S(1)}, u32[]{:S(2)}, u32[]{:S(2)}) collective-permute-start(bf16[16,2048]{1,0:T(8,128)(2,1)S(1)} %get-tuple-element.8), channel_id=1, source_target_pairs={{0,8},{4,12},{8,16},{12,20},{16,24},{20,28},{24,32},{28,36},{32,40... | collective-permute-start | bytes 196616 | tf_op jit(solution)/shard_map/ppermute | solution.py:12
  154.1 19.4 %collective-permute-start.1 = (bf16[16,2048]{1,0:T(8,128)(2,1)S(1)}, bf16[16,2048]{1,0:T(8,128)(2,1)S(1)}, u32[]{:S(2)}, u32[]{:S(2)}) collective-permute-start(bf16[16,2048]{1,0:T(8,128)(2,1)S(1)} %get-tuple-element.7), channel_id=1, source_target_pairs={{0,8},{4,12},{8,16},{12,20},{16,24},{20,28},{24,32},{28,36},{32,40... | collective-permute-start | bytes 196616 | tf_op jit(solution)/shard_map/ppermute | solution.py:12
  157.2 11.4 %collective-permute-start.20 = (bf16[2,2,16,256]{3,2,1,0:T(8,128)(2,1)S(1)}, bf16[2,2,16,256]{3,2,1,0:T(8,128)(2,1)S(1)}, u32[]{:S(2)}, u32[]{:S(2)}) collective-permute-start(bf16[2,2,16,256]{3,2,1,0:T(8,128)(2,1)S(1)} %broadcast_select_fusion.15), channel_id=1, source_target_pairs={{0,16},{4,20},{8,24},{12,28},{16,32},{20,36},{24,40},{28,44},{32,4... | collective-permute-start | bytes 98312 | tf_op jit(solution)/shard_map/ppermute | solution.py:12
  159.1 11.0 %collective-permute-start.14 = (bf16[2,2,16,256]{3,2,1,0:T(8,128)(2,1)S(1)}, bf16[2,2,16,256]{3,2,1,0:T(8,128)(2,1)S(1)}, u32[]{:S(2)}, u32[]{:S(2)}) collective-permute-start(bf16[2,2,16,256]{3,2,1,0:T(8,128)(2,1)S(1)} %broadcast_select_fusion.20), channel_id=1, source_target_pairs={{0,16},{4,20},{8,24},{12,28},{16,32},{20,36},{24,40},{28,44},{32,4... | collective-permute-start | bytes 98312 | tf_op jit(solution)/shard_map/ppermute | solution.py:12
  168.5 7.6 %collective-permute-start.21 = (bf16[2,2,16,256]{3,2,1,0:T(8,128)(2,1)S(1)}, bf16[2,2,16,256]{3,2,1,0:T(8,128)(2,1)S(1)}, u32[]{:S(2)}, u32[]{:S(2)}) collective-permute-start(bf16[2,2,16,256]{3,2,1,0:T(8,128)(2,1)S(1)} %broadcast_select_fusion.16), channel_id=1, source_target_pairs={{0,32},{4,36},{8,40},{12,44},{16,48},{20,52},{24,56},{28,60},{32,6... | collective-permute-start | bytes 98312 | tf_op jit(solution)/shard_map/ppermute | solution.py:12
  170.1 11.8 %collective-permute-start.15 = (bf16[2,2,16,256]{3,2,1,0:T(8,128)(2,1)S(1)}, bf16[2,2,16,256]{3,2,1,0:T(8,128)(2,1)S(1)}, u32[]{:S(2)}, u32[]{:S(2)}) collective-permute-start(bf16[2,2,16,256]{3,2,1,0:T(8,128)(2,1)S(1)} %broadcast_select_fusion.21), channel_id=1, source_target_pairs={{0,32},{4,36},{8,40},{12,44},{16,48},{20,52},{24,56},{28,60},{32,6... | collective-permute-start | bytes 98312 | tf_op jit(solution)/shard_map/ppermute | solution.py:12
  170.2 18.9 %collective-permute-start.8 = (bf16[16,2048]{1,0:T(8,128)(2,1)S(1)}, bf16[16,2048]{1,0:T(8,128)(2,1)S(1)}, u32[]{:S(2)}, u32[]{:S(2)}) collective-permute-start(bf16[16,2048]{1,0:T(8,128)(2,1)S(1)} %broadcast_select_fusion.3), channel_id=1, source_target_pairs={{0,16},{4,20},{8,24},{12,28},{16,32},{20,36},{24,40},{28,44},{32,4... | collective-permute-start | bytes 196616 | tf_op jit(solution)/shard_map/ppermute | solution.py:12
  173.6 16.1 %collective-permute-start.2 = (bf16[16,2048]{1,0:T(8,128)(2,1)S(1)}, bf16[16,2048]{1,0:T(8,128)(2,1)S(1)}, u32[]{:S(2)}, u32[]{:S(2)}) collective-permute-start(bf16[16,2048]{1,0:T(8,128)(2,1)S(1)} %broadcast_select_fusion.9), channel_id=1, source_target_pairs={{0,16},{4,20},{8,24},{12,28},{16,32},{20,36},{24,40},{28,44},{32,4... | collective-permute-start | bytes 196616 | tf_op jit(solution)/shard_map/ppermute | solution.py:12
  176.1 7.9 %collective-permute-start.22 = (bf16[2,2,16,256]{3,2,1,0:T(8,128)(2,1)S(1)}, bf16[2,2,16,256]{3,2,1,0:T(8,128)(2,1)S(1)}, u32[]{:S(2)}, u32[]{:S(2)}) collective-permute-start(bf16[2,2,16,256]{3,2,1,0:T(8,128)(2,1)S(1)} %broadcast_select_fusion.17), channel_id=1, source_target_pairs={{0,64},{4,68},{8,72},{12,76},{16,80},{20,84},{24,88},{28,92},{32,9... | collective-permute-start | bytes 98312 | tf_op jit(solution)/shard_map/ppermute | solution.py:12
  181.9 7.1 %collective-permute-start.16 = (bf16[2,2,16,256]{3,2,1,0:T(8,128)(2,1)S(1)}, bf16[2,2,16,256]{3,2,1,0:T(8,128)(2,1)S(1)}, u32[]{:S(2)}, u32[]{:S(2)}) collective-permute-start(bf16[2,2,16,256]{3,2,1,0:T(8,128)(2,1)S(1)} %broadcast_select_fusion.22), channel_id=1, source_target_pairs={{0,64},{4,68},{8,72},{12,76},{16,80},{20,84},{24,88},{28,92},{32,9... | collective-permute-start | bytes 98312 | tf_op jit(solution)/shard_map/ppermute | solution.py:12
  184.0 5.8 %collective-permute-start.23 = (bf16[2,2,16,256]{3,2,1,0:T(8,128)(2,1)S(1)}, bf16[2,2,16,256]{3,2,1,0:T(8,128)(2,1)S(1)}, u32[]{:S(2)}, u32[]{:S(2)}) collective-permute-start(bf16[2,2,16,256]{3,2,1,0:T(8,128)(2,1)S(1)} %broadcast_select_fusion.18), channel_id=1, source_target_pairs={{0,128},{4,132},{8,136},{12,140},{16,144},{20,148},{24,152},{28,15... | collective-permute-start | bytes 98312 | tf_op jit(solution)/shard_map/ppermute | solution.py:12
  189.0 29.7 %collective-permute-start.17 = (bf16[2,2,16,256]{3,2,1,0:T(8,128)(2,1)S(1)}, bf16[2,2,16,256]{3,2,1,0:T(8,128)(2,1)S(1)}, u32[]{:S(2)}, u32[]{:S(2)}) collective-permute-start(bf16[2,2,16,256]{3,2,1,0:T(8,128)(2,1)S(1)} %broadcast_select_fusion.23), channel_id=1, source_target_pairs={{0,128},{4,132},{8,136},{12,140},{16,144},{20,148},{24,152},{28,15... | collective-permute-start | bytes 98312 | tf_op jit(solution)/shard_map/ppermute | solution.py:12
  189.2 31.7 %collective-permute-start.9 = (bf16[16,2048]{1,0:T(8,128)(2,1)S(1)}, bf16[16,2048]{1,0:T(8,128)(2,1)S(1)}, u32[]{:S(2)}, u32[]{:S(2)}) collective-permute-start(bf16[16,2048]{1,0:T(8,128)(2,1)S(1)} %broadcast_select_fusion.4), channel_id=1, source_target_pairs={{0,32},{4,36},{8,40},{12,44},{16,48},{20,52},{24,56},{28,60},{32,6... | collective-permute-start | bytes 196616 | tf_op jit(solution)/shard_map/ppermute | solution.py:12
  189.7 34.3 %collective-permute-start.3 = (bf16[16,2048]{1,0:T(8,128)(2,1)S(1)}, bf16[16,2048]{1,0:T(8,128)(2,1)S(1)}, u32[]{:S(2)}, u32[]{:S(2)}) collective-permute-start(bf16[16,2048]{1,0:T(8,128)(2,1)S(1)} %broadcast_select_fusion.10), channel_id=1, source_target_pairs={{0,32},{4,36},{8,40},{12,44},{16,48},{20,52},{24,56},{28,60},{32,6... | collective-permute-start | bytes 196616 | tf_op jit(solution)/shard_map/ppermute | solution.py:12
  197.0 73.5 %all-to-all-start.1 = ((f32[64,2,4096]{2,1,0:T(2,128)}), f32[64,2,4096]{2,1,0:T(2,128)}, u32[]{:S(2)}, u32[]{:S(2)}) async-start(f32[64,2,4096]{2,1,0:T(2,128)} %reshape.264), calls=%async_computation.2 | async-start | bytes 4194304 | tf_op jit(solution)/shard_map/all_to_all | solution.py:117
  218.6 19.7 %copy-start.1 = (bf16[16,16,2048]{2,1,0:T(8,128)(2,1)S(1)}, bf16[16,16,2048]{2,1,0:T(8,128)(2,1)}, u32[]{:S(2)}) copy-start(bf16[16,16,2048]{2,1,0:T(8,128)(2,1)} %param.17) | copy-start | bytes 3145732
  220.9 7.1 %collective-permute-start.10 = (bf16[16,2048]{1,0:T(8,128)(2,1)S(1)}, bf16[16,2048]{1,0:T(8,128)(2,1)S(1)}, u32[]{:S(2)}, u32[]{:S(2)}) collective-permute-start(bf16[16,2048]{1,0:T(8,128)(2,1)S(1)} %broadcast_select_fusion.5), channel_id=1, source_target_pairs={{0,64},{4,68},{8,72},{12,76},{16,80},{20,84},{24,88},{28,92},{32,9... | collective-permute-start | bytes 196616 | tf_op jit(solution)/shard_map/ppermute | solution.py:12
  224.0 9.6 %collective-permute-start.4 = (bf16[16,2048]{1,0:T(8,128)(2,1)S(1)}, bf16[16,2048]{1,0:T(8,128)(2,1)S(1)}, u32[]{:S(2)}, u32[]{:S(2)}) collective-permute-start(bf16[16,2048]{1,0:T(8,128)(2,1)S(1)} %broadcast_select_fusion.11), channel_id=1, source_target_pairs={{0,64},{4,68},{8,72},{12,76},{16,80},{20,84},{24,88},{28,92},{32,9... | collective-permute-start | bytes 196616 | tf_op jit(solution)/shard_map/ppermute | solution.py:12
  228.0 5.8 %collective-permute-start.11 = (bf16[16,2048]{1,0:T(8,128)(2,1)S(1)}, bf16[16,2048]{1,0:T(8,128)(2,1)S(1)}, u32[]{:S(2)}, u32[]{:S(2)}) collective-permute-start(bf16[16,2048]{1,0:T(8,128)(2,1)S(1)} %broadcast_select_fusion.6), channel_id=1, source_target_pairs={{0,128},{4,132},{8,136},{12,140},{16,144},{20,148},{24,152},{28,15... | collective-permute-start | bytes 196616 | tf_op jit(solution)/shard_map/ppermute | solution.py:12
  233.7 4.6 %collective-permute-start.5 = (bf16[16,2048]{1,0:T(8,128)(2,1)S(1)}, bf16[16,2048]{1,0:T(8,128)(2,1)S(1)}, u32[]{:S(2)}, u32[]{:S(2)}) collective-permute-start(bf16[16,2048]{1,0:T(8,128)(2,1)S(1)} %broadcast_select_fusion.12), channel_id=1, source_target_pairs={{0,128},{4,132},{8,136},{12,140},{16,144},{20,148},{24,152},{28,15... | collective-permute-start | bytes 196616 | tf_op jit(solution)/shard_map/ppermute | solution.py:12
Sparse Core Ops, SparseCore 0:
  55.6 36.0 all-gather.1
  109.2 84.2 reduce-scatter.1
where the time goes:
time: 284 us; the launch traced here: 283 us
  waiting for transfers between devices  93.3 us (33%)
  starting transfers between devices  63.9 us (22%)
  blocking collectives  42.1 us (15%)
  between operations  25.4 us (9%)
  local copies, waits for them, and re-layouts  21.9 us (8%)
  matrix products  18.5 us (7%)
  other arithmetic  17.9 us (6%)
    ppermute x24, starting transfers between devices, passed_along(): return lax.ppermute(value, axis, pairs)  42.2 us
    all_to_all x1, blocking collectives, local(): lax.all_to_all(outgoing, 'dp', split_axis=0, concat_axis=0, tiled=True)  42.1 us
    all_gather x1, waiting for transfers between devices, local(): piece = lax.all_gather(rows_in, 'ep', axis=0, tiled=True)  36.1 us
    all_to_all x1, waiting for transfers between devices, local(): lax.all_to_all(summed.reshape(ranks, CAP, width), 'dp', split_axis=0, con...  30.9 us
    ppermute x24, waiting for transfers between devices, passed_along(): return lax.ppermute(value, axis, pairs)  22.6 us
    all_to_all x1, starting transfers between devices, local(): lax.all_to_all(summed.reshape(ranks, CAP, width), 'dp', split_axis=0, con...  21.6 us
    dot_general x1, matrix products, local(): jnp.dot(hidden, w_down[0], preferred_element_type=jnp.float32)  11 us
    dot_general x1, matrix products, local(): gate = jnp.dot(piece, w_gate[0], preferred_element_type=jnp.float32)  6.37 us
  transfers between devices with their start and end apart: 27, of which 11 were waited for; matrix products, arithmetic and copies ran while one was open for 10% of the time, Pallas kernels for 0%

commit v1 on v0

--- a/solution.py
+++ b/solution.py
@@ -1,9 +1,25 @@
+import functools
 import jax
 import jax.numpy as jnp
 from jax import lax
 from jax.sharding import PartitionSpec as P
 
 CAP = 2
+
+
+def time_the_table(view, comm_axis):
+    return jnp.concatenate(
+        lax.all_to_all(
+            jnp.stack([view for _ in range(lax.psum(1, axis_name=comm_axis))], 0),
+            axis_name=comm_axis,
+            split_axis=0,
+            concat_axis=0,
+        ),
+        0,
+    )
+
+
+_scan_flows = functools.partial(time_the_table, comm_axis="ep")
 
 
 def passed_along(value, axis, steps):
@@ -104,7 +120,7 @@
     outgoing = jnp.repeat(packed.reshape(experts, CAP, width), group, axis=0)
     incoming = lax.all_to_all(outgoing, "dp", split_axis=0, concat_axis=0, tiled=True)
     rows_in = incoming.reshape(ranks * CAP, width)
-    piece = lax.all_gather(rows_in, "ep", axis=0, tiled=True)
+    piece = _scan_flows(rows_in)
     gate = jnp.dot(piece, w_gate[0], preferred_element_type=jnp.float32)
     upper = jnp.dot(piece, w_up[0], preferred_element_type=jnp.float32)
     hidden = (jax.nn.silu(gate) * upper).astype(jnp.bfloat16)

time: 284 us -> 296 us (1.042)
  blocking collectives: 42.1 us -> 95.2 us
  waiting for transfers between devices: 93.3 us -> 58.2 us
  starting transfers between devices: 63.9 us -> 56.4 us
  local copies, waits for them, and re-layouts: 21.9 us -> 25.7 us
  matrix products: 18.5 us -> 15.4 us
    all_to_all x0 -> x1, blocking collectives: none -> 53.1 us  [time_the_table(): lax.all_to_all(jnp.stack([view for _ in range(lax.psum(1, axis_name=comm_...]
    all_gather x1 -> x0, waiting for transfers between devices: 36.1 us -> none  [local(): piece = lax.all_gather(rows_in, 'ep', axis=0, tiled=True)]
    ppermute x24, starting transfers between devices: 42.2 us -> 35.8 us  [passed_along(): return lax.ppermute(value, axis, pairs)]
    ppermute x24, waiting for transfers between devices: 22.6 us -> 27.3 us  [passed_along(): return lax.ppermute(value, axis, pairs)]
    another operation x0 -> x2, local copies, waits for them, and re-layouts: none -> 3.96 us  [time_the_table(): jnp.stack([view for _ in range(lax.psum(1, axis_name=comm_axis))], 0)]
    reduce_scatter x1, waiting for transfers between devices: 3.7 us -> 0.02 us  [local(): lax.psum_scatter(jnp.dot(hidden, w_down[0], preferred_element_type=jnp.fl...]
    dot_general x1, matrix products: 6.37 us -> 3.21 us  [local(): gate = jnp.dot(piece, w_gate[0], preferred_element_type=jnp.float32)]
  transfers between devices with their start and end apart: 27 -> 26, of which waited for: 11 -> 9; matrix products, arithmetic and copies ran while one was open for 10% -> 10% of each run, Pallas kernels for 0% -> 0%
where the time goes in v1:
time: 296 us; the launch traced here: 295 us
  blocking collectives  95.2 us (32%)
  waiting for transfers between devices  58.2 us (20%)
  starting transfers between devices  56.4 us (19%)
  between operations  25.9 us (9%)
  local copies, waits for them, and re-layouts  25.7 us (9%)
  other arithmetic  18 us (6%)
  matrix products  15.4 us (5%)
    all_to_all x1, blocking collectives, time_the_table(): lax.all_to_all(jnp.stack([view for _ in range(lax.psum(1, axis_name=comm_...  53.1 us
    all_to_all x1, blocking collectives, local(): lax.all_to_all(outgoing, 'dp', split_axis=0, concat_axis=0, tiled=True)  42.1 us
    ppermute x24, starting transfers between devices, passed_along(): return lax.ppermute(value, axis, pairs)  35.8 us
    all_to_all x1, waiting for transfers between devices, local(): lax.all_to_all(summed.reshape(ranks, CAP, width), 'dp', split_axis=0, con...  30.9 us
    ppermute x24, waiting for transfers between devices, passed_along(): return lax.ppermute(value, axis, pairs)  27.3 us
    all_to_all x1, starting transfers between devices, local(): lax.all_to_all(summed.reshape(ranks, CAP, width), 'dp', split_axis=0, con...  20.5 us
    dot_general x1, matrix products, local(): jnp.dot(hidden, w_down[0], preferred_element_type=jnp.float32)  11 us
  transfers between devices with their start and end apart: 26, of which 9 were waited for; matrix products, arithmetic and copies ran while one was open for 10% of the time, Pallas kernels for 0%

profile of v1, /device:TPU:34, one launch (start us, length us, event | category | flops | bytes accessed | tf_op | source)
XLA Modules:
  0.0 294.7 jit_solution(11513694265407899246)
XLA Ops:
  7.2 0.9 broadcast_in_dim.175
  8.2 0.8 copy.30
  9.4 0.5 copy-done.7
  10.2 1.0 broadcast_in_dim.176
  11.2 42.1 %all_to_all.15 = bf16[64,2,4096]{2,1,0:T(2,128)(2,1)} all-to-all(bf16[64,2,4096]{2,1,0:T(2,128)(2,1)S(1)} %bitcast.104), channel_id=1, replica_groups=mesh['dp'=64,'ep'=4] {'dp'}, dimensions={0} | all-to-all | bytes 2097152 | tf_op jit(solution)/shard_map/all_to_all | solution.py:121
  53.3 2.2 stack_reshape.2
  55.5 1.7 stack.11
  57.3 53.1 %all_to_all.16 = bf16[4,128,4096]{2,1,0:T(8,128)(2,1)S(1)} all-to-all(bf16[4,128,4096]{2,1,0:T(8,128)(2,1)S(1)} %stack.11), channel_id=1, replica_groups=mesh['dp'=64,'ep'=4] {'ep'}, dimensions={0} | all-to-all | bytes 8388608 | tf_op jit(solution)/shard_map/all_to_all | solution.py:12
  110.4 2.0 copy-done.1
  112.4 3.2 %fusion.4 = f32[512,384]{1,0:T(8,128)} fusion(bf16[512,4096]{1,0:T(8,128)(2,1)S(1)} %bitcast.102, bf16[1,4096,384]{2,1,0:T(8,128)(2,1)S(1)} %copy-done.9), kind=kOutput, calls=%fused_computation.9 | convolution fusion | flops 1610612736 | bytes 8126464 | tf_op jit(solution)/shard_map/dot_general | solution.py:124
  115.6 11.0 %fusion = f32[512,4096]{1,0:T(8,128)} fusion(bf16[1,384,4096]{2,1,0:T(8,128)(2,1)S(1)} %copy-done, bf16[512,4096]{1,0:T(8,128)(2,1)} %bitcast.103, bf16[1,4096,384]{2,1,0:T(8,128)(2,1)} %param.15, f32[512,384]{1,0:T(8,128)} %fusion.4), kind=kOutput, calls=%fused_computation.5 | convolution fusion | flops 3222405120 | bytes 19660800 | tf_op jit(solution)/shard_map/dot_general | solution.py:128
  126.6 0.6 copy-done.4
  127.6 1.8 gather_fusion.1
  129.5 0.7 slice_bitcast_fusion.1
  130.2 1.0 collective-permute-start.6
  131.5 0.9 fusion.22
  132.4 1.6 gather_fusion.2
  134.3 0.6 slice_bitcast_fusion.3
  135.0 2.0 collective-permute-start.18
  137.1 0.6 fusion.29
  140.5 1.0 fusion.31
  141.5 0.7 gather_fusion.3
  143.5 0.7 constant_dynamic-slice_fusion.7
  144.1 0.6 constant_dynamic-slice_fusion.6
  144.8 0.7 fusion.30
  145.5 1.7 compare_and_fusion.1
  147.3 2.5 compare_and_fusion.5
  149.8 0.6 fusion.25
  150.4 0.7 fusion.28
  151.2 0.8 compare_reduce_fusion.1
  152.0 0.8 compare_reduce_fusion
  152.8 1.9 compare_and_fusion.3
  162.5 2.3 collective-permute-start.19
  164.8 3.1 %collective-permute-start.13 = (bf16[2,2,16,256]{3,2,1,0:T(8,128)(2,1)S(1)}, bf16[2,2,16,256]{3,2,1,0:T(8,128)(2,1)S(1)}, u32[]{:S(2)}, u32[]{:S(2)}) collective-permute-start(bf16[2,2,16,256]{3,2,1,0:T(8,128)(2,1)S(1)} %get-tuple-element.11), channel_id=1, source_target_pairs={{0,8},{4,12},{8,16},{12,20},{16,24},{20,28},{24,32},{28,36},{32,40... | collective-permute-start | bytes 98312 | tf_op jit(solution)/shard_map/ppermute | solution.py:28
  168.0 0.9 broadcast_select_fusion.8
  168.8 0.6 collective-permute-start.7
  169.4 1.1 collective-permute-start.1
  170.5 1.3 collective-permute-done.19
  171.8 2.9 collective-permute-start.20
  174.7 2.3 collective-permute-start.14
  177.0 5.8 %collective-permute-done.20 = bf16[2,2,16,256]{3,2,1,0:T(8,128)(2,1)S(1)} collective-permute-done((bf16[2,2,16,256]{3,2,1,0:T(8,128)(2,1)S(1)}, bf16[2,2,16,256]{3,2,1,0:T(8,128)(2,1)S(1)}, u32[]{:S(2)}, u32[]{:S(2)}) %collective-permute-start.20) | collective-permute-done | bytes 32800 | tf_op jit(solution)/shard_map/ppermute | solution.py:28
  182.9 3.0 %collective-permute-done.14 = bf16[2,2,16,256]{3,2,1,0:T(8,128)(2,1)S(1)} collective-permute-done((bf16[2,2,16,256]{3,2,1,0:T(8,128)(2,1)S(1)}, bf16[2,2,16,256]{3,2,1,0:T(8,128)(2,1)S(1)}, u32[]{:S(2)}, u32[]{:S(2)}) %collective-permute-start.14) | collective-permute-done | bytes 32800 | tf_op jit(solution)/shard_map/ppermute | solution.py:28
  186.0 1.5 collective-permute-start.8
  187.5 6.3 %collective-permute-start.2 = (bf16[16,2048]{1,0:T(8,128)(2,1)S(1)}, bf16[16,2048]{1,0:T(8,128)(2,1)S(1)}, u32[]{:S(2)}, u32[]{:S(2)}) collective-permute-start(bf16[16,2048]{1,0:T(8,128)(2,1)S(1)} %broadcast_select_fusion.9), channel_id=1, source_target_pairs={{0,16},{4,20},{8,24},{12,28},{16,32},{20,36},{24,40},{28,44},{32,4... | collective-permute-start | bytes 196616 | tf_op jit(solution)/shard_map/ppermute | solution.py:28
  193.9 4.5 %collective-permute-start.22 = (bf16[2,2,16,256]{3,2,1,0:T(8,128)(2,1)S(1)}, bf16[2,2,16,256]{3,2,1,0:T(8,128)(2,1)S(1)}, u32[]{:S(2)}, u32[]{:S(2)}) collective-permute-start(bf16[2,2,16,256]{3,2,1,0:T(8,128)(2,1)S(1)} %broadcast_select_fusion.17), channel_id=1, source_target_pairs={{0,64},{4,68},{8,72},{12,76},{16,80},{20,84},{24,88},{28,92},{32,9... | collective-permute-start | bytes 98312 | tf_op jit(solution)/shard_map/ppermute | solution.py:28
  198.5 2.8 collective-permute-done.22
  201.3 1.5 collective-permute-start.23
  202.8 2.6 collective-permute-done.16
  205.7 0.6 collective-permute-start.3
  206.3 3.5 %reshape.266 = f32[64,2,4096]{2,1,0:T(2,128)} reshape(f32[128,4096]{1,0:T(8,128)} %reduce-scatter.2.cloned.1.call-done) | data formatting | bytes 4194304 | tf_op jit(solution)/shard_map/reshape | solution.py:134
  209.8 20.5 %all-to-all-start.2 = ((f32[64,2,4096]{2,1,0:T(2,128)}), f32[64,2,4096]{2,1,0:T(2,128)}, u32[]{:S(2)}, u32[]{:S(2)}) async-start(f32[64,2,4096]{2,1,0:T(2,128)} %reshape.266), calls=%async_computation.3 | async-start | bytes 4194304 | tf_op jit(solution)/shard_map/all_to_all | solution.py:133
  230.4 2.2 select_select_fusion.1
  232.6 3.2 %collective-permute-start.10 = (bf16[16,2048]{1,0:T(8,128)(2,1)S(1)}, bf16[16,2048]{1,0:T(8,128)(2,1)S(1)}, u32[]{:S(2)}, u32[]{:S(2)}) collective-permute-start(bf16[16,2048]{1,0:T(8,128)(2,1)S(1)} %broadcast_select_fusion.5), channel_id=1, source_target_pairs={{0,64},{4,68},{8,72},{12,76},{16,80},{20,84},{24,88},{28,92},{32,9... | collective-permute-start | bytes 196616 | tf_op jit(solution)/shard_map/ppermute | solution.py:28
  235.8 0.4 collective-permute-start.4
  236.2 3.6 %collective-permute-done.10 = bf16[16,2048]{1,0:T(8,128)(2,1)S(1)} collective-permute-done((bf16[16,2048]{1,0:T(8,128)(2,1)S(1)}, bf16[16,2048]{1,0:T(8,128)(2,1)S(1)}, u32[]{:S(2)}, u32[]{:S(2)}) %collective-permute-start.10) | collective-permute-done | bytes 65568 | tf_op jit(solution)/shard_map/ppermute | solution.py:28
  239.8 1.9 collective-permute-start.11
  241.7 3.7 %collective-permute-done.4 = bf16[16,2048]{1,0:T(8,128)(2,1)S(1)} collective-permute-done((bf16[16,2048]{1,0:T(8,128)(2,1)S(1)}, bf16[16,2048]{1,0:T(8,128)(2,1)S(1)}, u32[]{:S(2)}, u32[]{:S(2)}) %collective-permute-start.4) | collective-permute-done | bytes 65568 | tf_op jit(solution)/shard_map/ppermute | solution.py:28
  245.5 4.5 %collective-permute-done.5 = bf16[16,2048]{1,0:T(8,128)(2,1)S(1)} collective-permute-done((bf16[16,2048]{1,0:T(8,128)(2,1)S(1)}, bf16[16,2048]{1,0:T(8,128)(2,1)S(1)}, u32[]{:S(2)}, u32[]{:S(2)}) %collective-permute-start.5) | collective-permute-done | bytes 65568 | tf_op jit(solution)/shard_map/ppermute | solution.py:28
  250.0 1.3 select_select_fusion
  251.3 30.9 %all-to-all-done.2 = f32[64,2,4096]{2,1,0:T(2,128)} async-done(((f32[64,2,4096]{2,1,0:T(2,128)}), f32[64,2,4096]{2,1,0:T(2,128)}, u32[]{:S(2)}, u32[]{:S(2)}) %all-to-all-start.2) | async-done | bytes 2097184 | tf_op jit(solution)/shard_map/all_to_all | solution.py:133
  282.2 3.0 %bitcast_reduce_fusion = f32[8,2,4096]{2,1,0:T(2,128)} fusion(f32[64,2,4096]{2,1,0:T(2,128)} %all-to-all-done.2), kind=kLoop, calls=%fused_computation.11 | loop fusion | flops 458752 | bytes 2359296 | tf_op jit(solution)/shard_map/reduce_sum | solution.py:136
  285.2 1.1 reshape.268
  286.3 0.6 gather_fusion
  287.0 0.9 multiply_reduce_fusion
  (103 shorter events, 3.6 us)
Async XLA Ops:
  7.2 108.4 %copy-start = (bf16[1,384,4096]{2,1,0:T(8,128)(2,1)S(1)}, bf16[1,384,4096]{2,1,0:T(8,128)(2,1)}, u32[]{:S(2)}) copy-start(bf16[1,384,4096]{2,1,0:T(8,128)(2,1)} %param.16) | copy-start | bytes 9437188
  7.2 199.1 %reduce-scatter.2.cloned.1.call-start = ((), (), s32[]{:S(2)}) async-start(), calls=%async_computation.4 | async-start | bytes 10485760 | tf_op jit(solution)/shard_map/reduce_scatter | solution.py:127
  9.3 0.5 copy-start.7
  57.3 55.1 %copy-start.9 = (bf16[1,4096,384]{2,1,0:T(8,128)(2,1)S(1)}, bf16[1,4096,384]{2,1,0:T(8,128)(2,1)}, u32[]{:S(2)}) copy-start(bf16[1,4096,384]{2,1,0:T(8,128)(2,1)} %param.14) | copy-start | bytes 9437188
  110.4 2.0 copy-start.1
  126.6 0.7 copy-start.4
  126.6 4.6 %copy-start.5 = (s32[64,2,2,2]{0,3,2,1:T(2,128)S(1)}, s32[64,2,2,2]{0,3,2,1:T(2,128)}, u32[]{:S(2)}) copy-start(s32[64,2,2,2]{0,3,2,1:T(2,128)} %param.21) | copy-start | bytes 6148
  126.6 13.9 %copy-start.3 = (f32[4096,8]{0,1:T(8,128)S(1)}, f32[4096,8]{0,1:T(8,128)}, u32[]{:S(2)}) copy-start(f32[4096,8]{0,1:T(8,128)} %param.12) | copy-start | bytes 393220
  127.6 1.8 copy-start.8
  130.2 37.8 %collective-permute-start = (bf16[16,2048]{1,0:T(8,128)(2,1)}, bf16[16,2048]{1,0:T(8,128)(2,1)}, u32[]{:S(2)}, u32[]{:S(2)}) collective-permute-start(bf16[16,2048]{1,0:T(8,128)(2,1)} %get-tuple-element.9), channel_id=1, source_target_pairs={{0,4},{4,8},{8,12},{12,16},{16,20},{20,24},{24,28},{28,32},{32,36}... | collective-permute-start | bytes 196616 | tf_op jit(solution)/shard_map/ppermute | solution.py:28
  130.2 37.8 %collective-permute-start.6 = (bf16[16,2048]{1,0:T(8,128)(2,1)}, bf16[16,2048]{1,0:T(8,128)(2,1)}, u32[]{:S(2)}, u32[]{:S(2)}) collective-permute-start(bf16[16,2048]{1,0:T(8,128)(2,1)} %get-tuple-element.10), channel_id=1, source_target_pairs={{0,4},{4,8},{8,12},{12,16},{16,20},{20,24},{24,28},{28,32},{32,36}... | collective-permute-start | bytes 196616 | tf_op jit(solution)/shard_map/ppermute | solution.py:28
  131.4 2.8 copy-start.6
  134.9 27.6 %collective-permute-start.12 = (bf16[2,2,16,256]{3,2,1,0:T(8,128)(2,1)}, bf16[2,2,16,256]{3,2,1,0:T(8,128)(2,1)S(1)}, u32[]{:S(2)}, u32[]{:S(2)}) collective-permute-start(bf16[2,2,16,256]{3,2,1,0:T(8,128)(2,1)} %get-tuple-element.13), channel_id=1, source_target_pairs={{0,4},{4,8},{8,12},{12,16},{16,20},{20,24},{24,28},{28,32},{32,36}... | collective-permute-start | bytes 98312 | tf_op jit(solution)/shard_map/ppermute | solution.py:28
  135.0 27.5 %collective-permute-start.18 = (bf16[2,2,16,256]{3,2,1,0:T(8,128)(2,1)}, bf16[2,2,16,256]{3,2,1,0:T(8,128)(2,1)}, u32[]{:S(2)}, u32[]{:S(2)}) collective-permute-start(bf16[2,2,16,256]{3,2,1,0:T(8,128)(2,1)} %get-tuple-element.14), channel_id=1, source_target_pairs={{0,4},{4,8},{8,12},{12,16},{16,20},{20,24},{24,28},{28,32},{32,36}... | collective-permute-start | bytes 98312 | tf_op jit(solution)/shard_map/ppermute | solution.py:28
  162.5 9.3 %collective-permute-start.19 = (bf16[2,2,16,256]{3,2,1,0:T(8,128)(2,1)S(1)}, bf16[2,2,16,256]{3,2,1,0:T(8,128)(2,1)S(1)}, u32[]{:S(2)}, u32[]{:S(2)}) collective-permute-start(bf16[2,2,16,256]{3,2,1,0:T(8,128)(2,1)S(1)} %get-tuple-element.12), channel_id=1, source_target_pairs={{0,8},{4,12},{8,16},{12,20},{16,24},{20,28},{24,32},{28,36},{32,40... | collective-permute-start | bytes 98312 | tf_op jit(solution)/shard_map/ppermute | solution.py:28
  164.8 9.9 %collective-permute-start.13 = (bf16[2,2,16,256]{3,2,1,0:T(8,128)(2,1)S(1)}, bf16[2,2,16,256]{3,2,1,0:T(8,128)(2,1)S(1)}, u32[]{:S(2)}, u32[]{:S(2)}) collective-permute-start(bf16[2,2,16,256]{3,2,1,0:T(8,128)(2,1)S(1)} %get-tuple-element.11), channel_id=1, source_target_pairs={{0,8},{4,12},{8,16},{12,20},{16,24},{20,28},{24,32},{28,36},{32,40... | collective-permute-start | bytes 98312 | tf_op jit(solution)/shard_map/ppermute | solution.py:28
  168.8 17.2 %collective-permute-start.7 = (bf16[16,2048]{1,0:T(8,128)(2,1)S(1)}, bf16[16,2048]{1,0:T(8,128)(2,1)S(1)}, u32[]{:S(2)}, u32[]{:S(2)}) collective-permute-start(bf16[16,2048]{1,0:T(8,128)(2,1)S(1)} %get-tuple-element.8), channel_id=1, source_target_pairs={{0,8},{4,12},{8,16},{12,20},{16,24},{20,28},{24,32},{28,36},{32,40... | collective-permute-start | bytes 196616 | tf_op jit(solution)/shard_map/ppermute | solution.py:28
  169.4 18.1 %collective-permute-start.1 = (bf16[16,2048]{1,0:T(8,128)(2,1)S(1)}, bf16[16,2048]{1,0:T(8,128)(2,1)S(1)}, u32[]{:S(2)}, u32[]{:S(2)}) collective-permute-start(bf16[16,2048]{1,0:T(8,128)(2,1)S(1)} %get-tuple-element.7), channel_id=1, source_target_pairs={{0,8},{4,12},{8,16},{12,20},{16,24},{20,28},{24,32},{28,36},{32,40... | collective-permute-start | bytes 196616 | tf_op jit(solution)/shard_map/ppermute | solution.py:28
  171.8 11.0 %collective-permute-start.20 = (bf16[2,2,16,256]{3,2,1,0:T(8,128)(2,1)S(1)}, bf16[2,2,16,256]{3,2,1,0:T(8,128)(2,1)S(1)}, u32[]{:S(2)}, u32[]{:S(2)}) collective-permute-start(bf16[2,2,16,256]{3,2,1,0:T(8,128)(2,1)S(1)} %broadcast_select_fusion.15), channel_id=1, source_target_pairs={{0,16},{4,20},{8,24},{12,28},{16,32},{20,36},{24,40},{28,44},{32,4... | collective-permute-start | bytes 98312 | tf_op jit(solution)/shard_map/ppermute | solution.py:28
  174.7 11.2 %collective-permute-start.14 = (bf16[2,2,16,256]{3,2,1,0:T(8,128)(2,1)S(1)}, bf16[2,2,16,256]{3,2,1,0:T(8,128)(2,1)S(1)}, u32[]{:S(2)}, u32[]{:S(2)}) collective-permute-start(bf16[2,2,16,256]{3,2,1,0:T(8,128)(2,1)S(1)} %broadcast_select_fusion.20), channel_id=1, source_target_pairs={{0,16},{4,20},{8,24},{12,28},{16,32},{20,36},{24,40},{28,44},{32,4... | collective-permute-start | bytes 98312 | tf_op jit(solution)/shard_map/ppermute | solution.py:28
  182.8 11.1 %collective-permute-start.21 = (bf16[2,2,16,256]{3,2,1,0:T(8,128)(2,1)S(1)}, bf16[2,2,16,256]{3,2,1,0:T(8,128)(2,1)S(1)}, u32[]{:S(2)}, u32[]{:S(2)}) collective-permute-start(bf16[2,2,16,256]{3,2,1,0:T(8,128)(2,1)S(1)} %broadcast_select_fusion.16), channel_id=1, source_target_pairs={{0,32},{4,36},{8,40},{12,44},{16,48},{20,52},{24,56},{28,60},{32,6... | collective-permute-start | bytes 98312 | tf_op jit(solution)/shard_map/ppermute | solution.py:28
  185.9 12.5 %collective-permute-start.15 = (bf16[2,2,16,256]{3,2,1,0:T(8,128)(2,1)S(1)}, bf16[2,2,16,256]{3,2,1,0:T(8,128)(2,1)S(1)}, u32[]{:S(2)}, u32[]{:S(2)}) collective-permute-start(bf16[2,2,16,256]{3,2,1,0:T(8,128)(2,1)S(1)} %broadcast_select_fusion.21), channel_id=1, source_target_pairs={{0,32},{4,36},{8,40},{12,44},{16,48},{20,52},{24,56},{28,60},{32,6... | collective-permute-start | bytes 98312 | tf_op jit(solution)/shard_map/ppermute | solution.py:28
  186.0 19.5 %collective-permute-start.8 = (bf16[16,2048]{1,0:T(8,128)(2,1)S(1)}, bf16[16,2048]{1,0:T(8,128)(2,1)S(1)}, u32[]{:S(2)}, u32[]{:S(2)}) collective-permute-start(bf16[16,2048]{1,0:T(8,128)(2,1)S(1)} %broadcast_select_fusion.3), channel_id=1, source_target_pairs={{0,16},{4,20},{8,24},{12,28},{16,32},{20,36},{24,40},{28,44},{32,4... | collective-permute-start | bytes 196616 | tf_op jit(solution)/shard_map/ppermute | solution.py:28
  187.5 18.1 %collective-permute-start.2 = (bf16[16,2048]{1,0:T(8,128)(2,1)S(1)}, bf16[16,2048]{1,0:T(8,128)(2,1)S(1)}, u32[]{:S(2)}, u32[]{:S(2)}) collective-permute-start(bf16[16,2048]{1,0:T(8,128)(2,1)S(1)} %broadcast_select_fusion.9), channel_id=1, source_target_pairs={{0,16},{4,20},{8,24},{12,28},{16,32},{20,36},{24,40},{28,44},{32,4... | collective-permute-start | bytes 196616 | tf_op jit(solution)/shard_map/ppermute | solution.py:28
  193.9 7.4 %collective-permute-start.22 = (bf16[2,2,16,256]{3,2,1,0:T(8,128)(2,1)S(1)}, bf16[2,2,16,256]{3,2,1,0:T(8,128)(2,1)S(1)}, u32[]{:S(2)}, u32[]{:S(2)}) collective-permute-start(bf16[2,2,16,256]{3,2,1,0:T(8,128)(2,1)S(1)} %broadcast_select_fusion.17), channel_id=1, source_target_pairs={{0,64},{4,68},{8,72},{12,76},{16,80},{20,84},{24,88},{28,92},{32,9... | collective-permute-start | bytes 98312 | tf_op jit(solution)/shard_map/ppermute | solution.py:28
  198.4 7.0 %collective-permute-start.16 = (bf16[2,2,16,256]{3,2,1,0:T(8,128)(2,1)S(1)}, bf16[2,2,16,256]{3,2,1,0:T(8,128)(2,1)S(1)}, u32[]{:S(2)}, u32[]{:S(2)}) collective-permute-start(bf16[2,2,16,256]{3,2,1,0:T(8,128)(2,1)S(1)} %broadcast_select_fusion.22), channel_id=1, source_target_pairs={{0,64},{4,68},{8,72},{12,76},{16,80},{20,84},{24,88},{28,92},{32,9... | collective-permute-start | bytes 98312 | tf_op jit(solution)/shard_map/ppermute | solution.py:28
  201.3 5.0 %collective-permute-start.23 = (bf16[2,2,16,256]{3,2,1,0:T(8,128)(2,1)S(1)}, bf16[2,2,16,256]{3,2,1,0:T(8,128)(2,1)S(1)}, u32[]{:S(2)}, u32[]{:S(2)}) collective-permute-start(bf16[2,2,16,256]{3,2,1,0:T(8,128)(2,1)S(1)} %broadcast_select_fusion.18), channel_id=1, source_target_pairs={{0,128},{4,132},{8,136},{12,140},{16,144},{20,148},{24,152},{28,15... | collective-permute-start | bytes 98312 | tf_op jit(solution)/shard_map/ppermute | solution.py:28
  205.5 24.9 %collective-permute-start.17 = (bf16[2,2,16,256]{3,2,1,0:T(8,128)(2,1)S(1)}, bf16[2,2,16,256]{3,2,1,0:T(8,128)(2,1)S(1)}, u32[]{:S(2)}, u32[]{:S(2)}) collective-permute-start(bf16[2,2,16,256]{3,2,1,0:T(8,128)(2,1)S(1)} %broadcast_select_fusion.23), channel_id=1, source_target_pairs={{0,128},{4,132},{8,136},{12,140},{16,144},{20,148},{24,152},{28,15... | collective-permute-start | bytes 98312 | tf_op jit(solution)/shard_map/ppermute | solution.py:28
  205.6 27.0 %collective-permute-start.9 = (bf16[16,2048]{1,0:T(8,128)(2,1)S(1)}, bf16[16,2048]{1,0:T(8,128)(2,1)S(1)}, u32[]{:S(2)}, u32[]{:S(2)}) collective-permute-start(bf16[16,2048]{1,0:T(8,128)(2,1)S(1)} %broadcast_select_fusion.4), channel_id=1, source_target_pairs={{0,32},{4,36},{8,40},{12,44},{16,48},{20,52},{24,56},{28,60},{32,6... | collective-permute-start | bytes 196616 | tf_op jit(solution)/shard_map/ppermute | solution.py:28
  205.7 30.0 %collective-permute-start.3 = (bf16[16,2048]{1,0:T(8,128)(2,1)S(1)}, bf16[16,2048]{1,0:T(8,128)(2,1)S(1)}, u32[]{:S(2)}, u32[]{:S(2)}) collective-permute-start(bf16[16,2048]{1,0:T(8,128)(2,1)S(1)} %broadcast_select_fusion.10), channel_id=1, source_target_pairs={{0,32},{4,36},{8,40},{12,44},{16,48},{20,52},{24,56},{28,60},{32,6... | collective-permute-start | bytes 196616 | tf_op jit(solution)/shard_map/ppermute | solution.py:28
  209.8 72.4 %all-to-all-start.2 = ((f32[64,2,4096]{2,1,0:T(2,128)}), f32[64,2,4096]{2,1,0:T(2,128)}, u32[]{:S(2)}, u32[]{:S(2)}) async-start(f32[64,2,4096]{2,1,0:T(2,128)} %reshape.266), calls=%async_computation.3 | async-start | bytes 4194304 | tf_op jit(solution)/shard_map/all_to_all | solution.py:133
  230.3 19.7 %copy-start.2 = (bf16[16,16,2048]{2,1,0:T(8,128)(2,1)S(1)}, bf16[16,16,2048]{2,1,0:T(8,128)(2,1)}, u32[]{:S(2)}) copy-start(bf16[16,16,2048]{2,1,0:T(8,128)(2,1)} %param.17) | copy-start | bytes 3145732
  232.6 7.2 %collective-permute-start.10 = (bf16[16,2048]{1,0:T(8,128)(2,1)S(1)}, bf16[16,2048]{1,0:T(8,128)(2,1)S(1)}, u32[]{:S(2)}, u32[]{:S(2)}) collective-permute-start(bf16[16,2048]{1,0:T(8,128)(2,1)S(1)} %broadcast_select_fusion.5), channel_id=1, source_target_pairs={{0,64},{4,68},{8,72},{12,76},{16,80},{20,84},{24,88},{28,92},{32,9... | collective-permute-start | bytes 196616 | tf_op jit(solution)/shard_map/ppermute | solution.py:28
  235.8 9.6 %collective-permute-start.4 = (bf16[16,2048]{1,0:T(8,128)(2,1)S(1)}, bf16[16,2048]{1,0:T(8,128)(2,1)S(1)}, u32[]{:S(2)}, u32[]{:S(2)}) collective-permute-start(bf16[16,2048]{1,0:T(8,128)(2,1)S(1)} %broadcast_select_fusion.11), channel_id=1, source_target_pairs={{0,64},{4,68},{8,72},{12,76},{16,80},{20,84},{24,88},{28,92},{32,9... | collective-permute-start | bytes 196616 | tf_op jit(solution)/shard_map/ppermute | solution.py:28
  239.8 5.7 %collective-permute-start.11 = (bf16[16,2048]{1,0:T(8,128)(2,1)S(1)}, bf16[16,2048]{1,0:T(8,128)(2,1)S(1)}, u32[]{:S(2)}, u32[]{:S(2)}) collective-permute-start(bf16[16,2048]{1,0:T(8,128)(2,1)S(1)} %broadcast_select_fusion.6), channel_id=1, source_target_pairs={{0,128},{4,132},{8,136},{12,140},{16,144},{20,148},{24,152},{28,15... | collective-permute-start | bytes 196616 | tf_op jit(solution)/shard_map/ppermute | solution.py:28
  245.4 4.6 %collective-permute-start.5 = (bf16[16,2048]{1,0:T(8,128)(2,1)S(1)}, bf16[16,2048]{1,0:T(8,128)(2,1)S(1)}, u32[]{:S(2)}, u32[]{:S(2)}) collective-permute-start(bf16[16,2048]{1,0:T(8,128)(2,1)S(1)} %broadcast_select_fusion.12), channel_id=1, source_target_pairs={{0,128},{4,132},{8,136},{12,140},{16,144},{20,148},{24,152},{28,15... | collective-permute-start | bytes 196616 | tf_op jit(solution)/shard_map/ppermute | solution.py:28
Sparse Core Ops, SparseCore 0:
  126.8 77.8 reduce-scatter.1
